TPU v7x, 32 devices: a whole 2x2x4 slice. The times are simulated.
32 devices in a mesh: mem: 4 (over y, core), sub: 8 (over z, x).
Axes of the slice: x: 2, y: 2, z: 4, core: 2. Of those that a mesh axis runs over, the one named last changes fastest.
Arguments:
- prior_sample_array: float32 [80, 8, 24, 512], P('mem', 'sub'), may hold values from -6 to 6
- courant_x: float32 [8, 512], P('sub'), may hold values from -0.3 to 0.3
- courant_y: float32 [8, 512], P('sub'), may hold values from -0.3 to 0.3
- diffusion: float32 [8, 512], P('sub'), may hold values from 0.02 to 0.09
- obs_cell: int32 [4, 128], replicated, may hold values from 0 to 4095
- obs_value: float32 [4, 128], replicated, may hold values from -6 to 6
- obs_error: float32 [4, 128], replicated, may hold values from 0.2 to 1
- obs_weight: float32 [4, 128, 24], replicated, may hold values from -1.25 to 1.25
- taper_radius: float32 [4, 128], replicated, may hold values from 64 to 256
Outputs:
- analysis: float32 [80, 8, 24, 512], P(None, 'sub', None, 'mem')
All inputs are finite; a program needn't handle non-finite values.
Results may differ from a plain program's by a relative error of at most 0.0003.
Values sent between devices are 32-bit elements; how exact they have to be, the bound alone decides.
No kernel may reach another device: no remote copies, remote signals or barrier semaphores. Data moves between devices by JAX's collectives and lax.ppermute only.
A program may use at most 64 MiB of HBM per device.

v0:
```python
import jax
import jax.numpy as jnp
from jax import lax
from jax.sharding import PartitionSpec as P

highest = lax.Precision.HIGHEST


def padded_2(shard, sides, width):
    for axis, dim in sides:
        size, length = (lax.axis_size(axis), shard.shape[dim])
        up = [(i, (i + 1) % size) for i in range(size - 1)]
        down = [(j, i) for i, j in up]
        last = lax.slice_in_dim(shard, length - width, length, axis=dim)
        first = lax.slice_in_dim(shard, 0, width, axis=dim)
        before = lax.ppermute(last, axis, up)
        after = lax.ppermute(first, axis, down)
        shard = jnp.concatenate([before, shard, after], axis=dim)
    return shard


def gaspari(delta_row, delta_col, cutoff_radius, width):
    cyclic_shifted = (delta_col + width // 2) % width - width // 2
    row_dist = delta_row.astype(jnp.float32)
    col_dist = cyclic_shifted.astype(jnp.float32)
    ratio = jnp.sqrt(row_dist * row_dist + col_dist * col_dist) / cutoff_radius
    inner = (((-0.25 * ratio + 0.5) * ratio + 0.625) * ratio - 5.0 / 3.0) * ratio * ratio + 1.0
    bounded = jnp.maximum(ratio, 1.0)
    outer = (
        ((((ratio / 12.0 - 0.5) * ratio + 0.625) * ratio + 5.0 / 3.0) * ratio - 5.0) * ratio
        + 4.0
        - 2.0 / (3.0 * bounded)
    )
    return jnp.where(ratio <= 1.0, inner, jnp.where(ratio < 2.0, outer, 0.0))


def carried_quantity(
    center,
    west_cells,
    east_cells,
    north_cells,
    southern_neighbours,
    flow_x,
    meridional_velocity,
    mixing,
):
    result = (
        center
        - jnp.maximum(flow_x, 0.0) * (center - west_cells)
        - jnp.minimum(flow_x, 0.0) * (east_cells - center)
    )
    result = (
        result
        - jnp.maximum(meridional_velocity, 0.0) * (center - southern_neighbours)
        - jnp.minimum(meridional_velocity, 0.0) * (north_cells - center)
    )
    return result + mixing * (
        east_cells + west_cells + north_cells + southern_neighbours - 4.0 * center
    )


def obs_factors(obs_prior, obs_value, obs_error):
    members = obs_prior.shape[1]
    average = jnp.mean(obs_prior, axis=1)
    anomaly = obs_prior - average[:, None]
    covariance = jnp.dot(anomaly, anomaly.T, precision=highest) / (members - 1) + jnp.diag(
        obs_error
    )
    factor = jnp.linalg.cholesky(covariance)
    innovation = (obs_value - average)[:, None]
    midpoint_values = lax.linalg.triangular_solve(factor, innovation, left_side=True, lower=True)
    solved = lax.linalg.triangular_solve(
        factor, midpoint_values, left_side=True, lower=True, transpose_a=True
    )
    shifted = factor + jnp.diag(jnp.sqrt(obs_error))
    reduced = lax.linalg.triangular_solve(shifted, anomaly, left_side=True, lower=True)
    squared = lax.linalg.triangular_solve(
        factor, reduced, left_side=True, lower=True, transpose_a=True
    )
    return (anomaly, solved - squared)


def local_prior(existing_grid_values, obs_rows, obs_cols, weights, row_start, col_start):
    rows_dev = existing_grid_values.shape[1]
    cols_dev = existing_grid_values.shape[3]
    local_rows = obs_rows - row_start
    local_cols = obs_cols - col_start
    owned = (
        (local_rows >= 0) & (local_rows < rows_dev) & (local_cols >= 0) & (local_cols < cols_dev)
    )
    picked = existing_grid_values[
        :, jnp.clip(local_rows, 0, rows_dev - 1), :, jnp.clip(local_cols, 0, cols_dev - 1)
    ]
    values = jnp.einsum("kmc,kc->km", picked, weights, precision=highest)
    return jnp.where(owned[:, None], values, 0.0)


def apply_update(existing_grid_values, obs_anomaly, coeffs, taper_cells, members):
    average = jnp.mean(existing_grid_values, axis=0)
    anomaly = existing_grid_values - average[None]
    cross_cov = jnp.einsum("mrcx,km->rcxk", anomaly, obs_anomaly, precision=highest) / (members - 1)
    gain = cross_cov * taper_cells[:, None, :, :]
    return existing_grid_values + jnp.einsum("rcxk,km->mrcx", gain, coeffs, precision=highest)


def shards(
    prior_sample_array,
    courant_x,
    courant_y,
    diffusion,
    obs_cell,
    obs_value,
    obs_error,
    obs_weight,
    taper_radius,
):
    width = courant_x.shape[1]
    rows_dev = prior_sample_array.shape[1]
    cols_dev = width // lax.axis_size("mem")
    members = prior_sample_array.shape[0] * lax.axis_size("mem")
    col_start = lax.axis_index("mem") * cols_dev
    row_start = lax.axis_index("sub") * rows_dev
    padded = padded_2(prior_sample_array, (("sub", 1),), 1)
    propagated_grids = carried_quantity(
        prior_sample_array,
        jnp.roll(prior_sample_array, 1, axis=3),
        jnp.roll(prior_sample_array, -1, axis=3),
        padded[:, 2:],
        padded[:, :-2],
        courant_x[:, None, :],
        courant_y[:, None, :],
        diffusion[:, None, :],
    )
    existing_grid_values = lax.all_to_all(
        propagated_grids, "mem", split_axis=3, concat_axis=0, tiled=True
    )
    row_ids = row_start + jnp.arange(rows_dev, dtype=jnp.int32)
    col_ids = col_start + jnp.arange(cols_dev, dtype=jnp.int32)
    obs_rows = obs_cell // width
    obs_cols = obs_cell % width
    batches = obs_cell.shape[0]

    def taper_cells(batch_index):
        return gaspari(
            row_ids[:, None, None] - obs_rows[batch_index][None, None, :],
            col_ids[None, :, None] - obs_cols[batch_index][None, None, :],
            taper_radius[batch_index][None, None, :],
            width,
        )

    for batch_index in range(batches):
        obs_prior = lax.psum(
            local_prior(
                existing_grid_values,
                obs_rows[batch_index],
                obs_cols[batch_index],
                obs_weight[batch_index],
                row_start,
                col_start,
            ),
            ("mem", "sub"),
        )
        obs_anomaly, coeffs = obs_factors(obs_prior, obs_value[batch_index], obs_error[batch_index])
        existing_grid_values = apply_update(
            existing_grid_values, obs_anomaly, coeffs, taper_cells(batch_index), members
        )
    return existing_grid_values


def solution(mesh):
    return jax.shard_map(
        shards,
        mesh=mesh,
        in_specs=(
            P("mem", "sub", None, None),
            P("sub", None),
            P("sub", None),
            P("sub", None),
            P(),
            P(),
            P(),
            P(),
            P(),
        ),
        out_specs=P(None, "sub", None, "mem"),
        check_vma=False,
    )
```

profile of v0, /device:TPU:0, one launch (start us, length us, event | category | flops | bytes accessed | tf_op | source)
XLA Modules:
  0.0 428.5 jit_solution(3687478982285887635)
XLA Ops:
  0.0 5.9 %collective-permute-start = (f32[20,1,24,512]{3,2,1,0:T(8,128)}, f32[20,1,24,512]{3,2,1,0:T(8,128)}, u32[]{:S(2)}, u32[]{:S(2)}) collective-permute-start(f32[20,1,24,512]{3,2,1,0:T(8,128)} %param.18), channel_id=1, source_target_pairs={{0,1},{1,2},{2,3},{3,4},{4,5},{5,6},{6,7},{8,9},{9,10},{10,11},{11... | collective-permute-start | bytes 2949128 | tf_op jit(solution)/shard_map/ppermute | solution.py:16
  14.5 32.9 %collective-permute-done = f32[20,1,24,512]{3,2,1,0:T(8,128)} collective-permute-done((f32[20,1,24,512]{3,2,1,0:T(8,128)}, f32[20,1,24,512]{3,2,1,0:T(8,128)}, u32[]{:S(2)}, u32[]{:S(2)}) %collective-permute-start) | collective-permute-done | bytes 983072 | tf_op jit(solution)/shard_map/ppermute | solution.py:16
  48.3 2.4 multiply_add_fusion
  50.7 4.3 copy.87
  54.9 6.5 %reshape.1524 = f32[4,1,61440]{2,1,0:T(1,128)} reshape(f32[512,1,20,24]{3,2,1,0:T(8,128)} %bitcast.330) | data formatting | bytes 1966080
  61.5 4.1 all-to-all-start
  68.4 10.9 %all-to-all-done = f32[4,1,61440]{2,1,0:T(1,128)S(1)} async-done(((f32[4,1,61440]{2,1,0:T(1,128)}), f32[4,1,61440]{2,1,0:T(1,128)S(1)}, u32[]{:S(2)}, u32[]{:S(2)}) %all-to-all-start) | async-done | bytes 983072 | tf_op jit(solution)/shard_map/all_to_all | solution.py:134
  79.8 3.5 reduce.20
  83.3 6.0 %reshape.1525 = f32[512,1,20,24]{3,2,1,0:T(8,128)} reshape(f32[4,61440]{1,0:T(4,128)S(1)} %reduce.20) | data formatting | bytes 1966080
  89.4 5.6 %copy.88 = f32[20,1,24,512]{3,1,2,0:T(1,128)S(1)} copy(f32[20,1,24,512]{2,0,1,3:T(8,128)} %bitcast.331) | data formatting | bytes 1966080 | tf_op jit(solution)/shard_map/all_to_all | solution.py:134
  99.2 41.8 %psum.28 = f32[128,80]{0,1:T(8,128)S(1)} all-reduce(f32[128,80]{0,1:T(8,128)S(1)} %broadcast_select_fusion.3), channel_id=1, replica_groups=mesh['mem'=4,'sub'=8] {'mem','sub'}, use_global_device_ids=true, to_apply=%region_0.1 | all-reduce | flops 10240 | bytes 81920 | tf_op jit(solution)/shard_map/psum | solution.py:152
  143.0 11.7 %cholesky.74 = f32[128,128]{1,0:T(8,128)S(1)} custom-call(f32[128,128]{1,0:T(8,128)S(1)} %copy.93), custom_call_target="Cholesky" | custom-call | tf_op jit(solution)/shard_map/jit(cholesky)/cholesky | solution.py:69
  156.1 9.8 %custom-call.36 = f32[1,128,128]{1,2,0:T(8,128)S(1)} custom-call(f32[1,128,128]{2,1,0:T(8,128)S(1)} %get-tuple-element.21), custom_call_target="InvertDiagBlocksLowerTriangular" | custom-call | tf_op jit(solution)/shard_map/triangular_solve/custom-call.3 | solution.py:76
  166.1 9.8 %custom-call.35 = f32[1,128,128]{1,2,0:T(8,128)S(1)} custom-call(f32[1,128,128]{2,1,0:T(8,128)S(1)} %get-tuple-element.20), custom_call_target="InvertDiagBlocksLowerTriangular" | custom-call | tf_op jit(solution)/shard_map/triangular_solve/custom-call.2 | solution.py:72
  176.4 2.6 fusion.31
  179.3 2.8 fusion.186
  184.5 40.4 %psum.29 = f32[128,80]{0,1:T(8,128)S(1)} all-reduce(f32[128,80]{0,1:T(8,128)S(1)} %broadcast_select_fusion.2), channel_id=1, replica_groups=mesh['mem'=4,'sub'=8] {'mem','sub'}, use_global_device_ids=true, to_apply=%region_5.11 | all-reduce | flops 10240 | bytes 81920 | tf_op jit(solution)/shard_map/psum | solution.py:152
  225.5 11.7 %cholesky.85 = f32[128,128]{1,0:T(8,128)S(1)} custom-call(f32[128,128]{1,0:T(8,128)S(1)} %copy.98), custom_call_target="Cholesky" | custom-call | tf_op jit(solution)/shard_map/jit(cholesky)/cholesky | solution.py:69
  238.7 9.8 %custom-call.40 = f32[1,128,128]{1,2,0:T(8,128)S(1)} custom-call(f32[1,128,128]{2,1,0:T(8,128)S(1)} %get-tuple-element.19), custom_call_target="InvertDiagBlocksLowerTriangular" | custom-call | tf_op jit(solution)/shard_map/triangular_solve/custom-call.3 | solution.py:76
  248.7 9.8 %custom-call.39 = f32[1,128,128]{1,2,0:T(8,128)S(1)} custom-call(f32[1,128,128]{2,1,0:T(8,128)S(1)} %get-tuple-element.18), custom_call_target="InvertDiagBlocksLowerTriangular" | custom-call | tf_op jit(solution)/shard_map/triangular_solve/custom-call.2 | solution.py:72
  258.9 2.6 fusion.37
  266.2 40.3 %psum.30 = f32[128,80]{0,1:T(8,128)S(1)} all-reduce(f32[128,80]{0,1:T(8,128)S(1)} %broadcast_select_fusion.1), channel_id=1, replica_groups=mesh['mem'=4,'sub'=8] {'mem','sub'}, use_global_device_ids=true, to_apply=%region_8.14 | all-reduce | flops 10240 | bytes 81920 | tf_op jit(solution)/shard_map/psum | solution.py:152
  307.1 11.7 %cholesky.96 = f32[128,128]{1,0:T(8,128)S(1)} custom-call(f32[128,128]{1,0:T(8,128)S(1)} %copy.101), custom_call_target="Cholesky" | custom-call | tf_op jit(solution)/shard_map/jit(cholesky)/cholesky | solution.py:69
  320.2 9.8 %custom-call.44 = f32[1,128,128]{1,2,0:T(8,128)S(1)} custom-call(f32[1,128,128]{2,1,0:T(8,128)S(1)} %get-tuple-element.17), custom_call_target="InvertDiagBlocksLowerTriangular" | custom-call | tf_op jit(solution)/shard_map/triangular_solve/custom-call.3 | solution.py:76
  330.2 9.8 %custom-call.43 = f32[1,128,128]{1,2,0:T(8,128)S(1)} custom-call(f32[1,128,128]{2,1,0:T(8,128)S(1)} %get-tuple-element.16), custom_call_target="InvertDiagBlocksLowerTriangular" | custom-call | tf_op jit(solution)/shard_map/triangular_solve/custom-call.2 | solution.py:72
  340.4 2.6 fusion.35
  343.3 1.9 fusion.188
  347.7 40.6 %psum.31 = f32[128,80]{0,1:T(8,128)S(1)} all-reduce(f32[128,80]{0,1:T(8,128)S(1)} %broadcast_select_fusion), channel_id=1, replica_groups=mesh['mem'=4,'sub'=8] {'mem','sub'}, use_global_device_ids=true, to_apply=%region_11.17 | all-reduce | flops 10240 | bytes 81920 | tf_op jit(solution)/shard_map/psum | solution.py:152
  388.9 11.7 %cholesky.107 = f32[128,128]{1,0:T(8,128)S(1)} custom-call(f32[128,128]{1,0:T(8,128)S(1)} %copy.104), custom_call_target="Cholesky" | custom-call | tf_op jit(solution)/shard_map/jit(cholesky)/cholesky | solution.py:69
  402.2 9.8 %custom-call.48 = f32[1,128,128]{1,2,0:T(8,128)S(1)} custom-call(f32[1,128,128]{2,1,0:T(8,128)S(1)} %get-tuple-element.15), custom_call_target="InvertDiagBlocksLowerTriangular" | custom-call | tf_op jit(solution)/shard_map/triangular_solve/custom-call.3 | solution.py:76
  412.2 9.8 %custom-call.47 = f32[1,128,128]{1,2,0:T(8,128)S(1)} custom-call(f32[1,128,128]{2,1,0:T(8,128)S(1)} %get-tuple-element.14), custom_call_target="InvertDiagBlocksLowerTriangular" | custom-call | tf_op jit(solution)/shard_map/triangular_solve/custom-call.2 | solution.py:72
  422.4 2.6 fusion.33
  (161 shorter events, 41.5 us)
Async XLA Ops:
  0.0 14.1 %copy-start.8 = (f32[20,1,24,512]{3,2,1,0:T(8,128)S(1)}, f32[20,1,24,512]{3,2,1,0:T(8,128)}, u32[]{:S(2)}) copy-start(f32[20,1,24,512]{3,2,1,0:T(8,128)} %param.18) | copy-start | bytes 2949124
  0.0 47.4 %collective-permute-start = (f32[20,1,24,512]{3,2,1,0:T(8,128)}, f32[20,1,24,512]{3,2,1,0:T(8,128)}, u32[]{:S(2)}, u32[]{:S(2)}) collective-permute-start(f32[20,1,24,512]{3,2,1,0:T(8,128)} %param.18), channel_id=1, source_target_pairs={{0,1},{1,2},{2,3},{3,4},{4,5},{5,6},{6,7},{8,9},{9,10},{10,11},{11... | collective-permute-start | bytes 2949128 | tf_op jit(solution)/shard_map/ppermute | solution.py:16
  5.9 41.4 %collective-permute-start.1 = (f32[20,1,24,512]{3,2,1,0:T(8,128)}, f32[20,1,24,512]{3,2,1,0:T(8,128)S(1)}, u32[]{:S(2)}, u32[]{:S(2)}) collective-permute-start(f32[20,1,24,512]{3,2,1,0:T(8,128)} %param.18), channel_id=1, source_target_pairs={{1,0},{2,1},{3,2},{4,3},{5,4},{6,5},{7,6},{9,8},{10,9},{11,10},{12... | collective-permute-start | bytes 2949128 | tf_op jit(solution)/shard_map/ppermute | solution.py:17
  14.1 34.2 %copy-start.15 = (f32[1,512]{1,0:T(1,128)S(1)}, f32[1,512]{1,0:T(1,128)}, u32[]{:S(2)}) copy-start(f32[1,512]{1,0:T(1,128)} %param.21) | copy-start | bytes 6148
  47.4 0.9 copy-start.10
  61.5 6.4 %copy-start.28 = (f32[4,128]{1,0:T(4,128)S(1)}, f32[4,128]{1,0:T(4,128)}, u32[]{:S(2)}) copy-start(f32[4,128]{1,0:T(4,128)} %param.26) | copy-start | bytes 6148
  61.5 17.8 %all-to-all-start = ((f32[4,1,61440]{2,1,0:T(1,128)}), f32[4,1,61440]{2,1,0:T(1,128)S(1)}, u32[]{:S(2)}, u32[]{:S(2)}) async-start(f32[4,1,61440]{2,1,0:T(1,128)} %reshape.1524), calls=%async_computation | async-start | bytes 1966080 | tf_op jit(solution)/shard_map/all_to_all | solution.py:134
  94.9 0.9 copy-start.9
  95.9 1.0 copy-start.6
  97.7 1.5 copy-start.19
  97.7 44.8 %copy-start.27 = (f32[128]{0:T(128)S(1)}, f32[128]{0:T(128)}, u32[]{:S(2)}) copy-start(f32[128]{0:T(128)} %get-tuple-element.52) | copy-start | bytes 1540
  97.7 57.7 %copy-start.26 = (f32[128]{0:T(128)S(1)}, f32[128]{0:T(128)}, u32[]{:S(2)}) copy-start(f32[128]{0:T(128)} %get-tuple-element.49) | copy-start | bytes 1540
  99.1 76.8 %copy-start.13 = (f32[4,128]{1,0:T(4,128)S(1)}, f32[4,128]{1,0:T(4,128)}, u32[]{:S(2)}) copy-start(f32[4,128]{1,0:T(4,128)} %param.23) | copy-start | bytes 6148
  99.1 77.2 %copy-start.7 = (f32[4,20,1,24,128]{4,3,1,0,2:T(8,128)S(1)}, f32[4,20,1,24,128]{4,3,1,0,2:T(8,128)}, u32[]{:S(2)}) copy-start(f32[4,20,1,24,128]{4,3,1,0,2:T(8,128)} %copy-done.6) | copy-start | bytes 2949124
  182.1 0.9 copy-start.2
  183.0 0.8 copy-start.11
  183.9 0.7 copy-start.18
  183.9 41.1 %copy-start.25 = (f32[128]{0:T(128)S(1)}, f32[128]{0:T(128)}, u32[]{:S(2)}) copy-start(f32[128]{0:T(128)} %get-tuple-element.51) | copy-start | bytes 1540
  183.9 54.1 %copy-start.24 = (f32[128]{0:T(128)S(1)}, f32[128]{0:T(128)}, u32[]{:S(2)}) copy-start(f32[128]{0:T(128)} %get-tuple-element.48) | copy-start | bytes 1540
  183.9 75.0 %copy-start.12 = (f32[24,128]{1,0:T(8,128)S(1)}, f32[24,128]{1,0:T(8,128)}, u32[]{:S(2)}) copy-start(f32[24,128]{1,0:T(8,128)} %get-tuple-element.64) | copy-start | bytes 36868
  183.9 75.0 %copy-start.3 = (f32[80,24,128]{2,0,1:T(8,128)S(1)}, f32[80,24,128]{2,0,1:T(8,128)}, u32[]{:S(2)}) copy-start(f32[80,24,128]{2,0,1:T(8,128)} %copy-done.2) | copy-start | bytes 2949124
  263.7 0.9 copy-start.4
  265.5 0.7 copy-start.17
  265.5 41.0 %copy-start.23 = (f32[128]{0:T(128)S(1)}, f32[128]{0:T(128)}, u32[]{:S(2)}) copy-start(f32[128]{0:T(128)} %get-tuple-element.53) | copy-start | bytes 1540
  265.5 54.0 %copy-start.22 = (f32[128]{0:T(128)S(1)}, f32[128]{0:T(128)}, u32[]{:S(2)}) copy-start(f32[128]{0:T(128)} %get-tuple-element.47) | copy-start | bytes 1540
  265.5 74.9 %copy-start.5 = (f32[80,24,128]{2,0,1:T(8,128)S(1)}, f32[80,24,128]{2,0,1:T(8,128)}, u32[]{:S(2)}) copy-start(f32[80,24,128]{2,0,1:T(8,128)} %copy-done.4) | copy-start | bytes 2949124
  345.3 0.9 copy-start
  347.1 0.7 copy-start.16
  347.1 41.3 %copy-start.21 = (f32[128]{0:T(128)S(1)}, f32[128]{0:T(128)}, u32[]{:S(2)}) copy-start(f32[128]{0:T(128)} %get-tuple-element.50) | copy-start | bytes 1540
  347.1 54.3 %copy-start.20 = (f32[128]{0:T(128)S(1)}, f32[128]{0:T(128)}, u32[]{:S(2)}) copy-start(f32[128]{0:T(128)} %get-tuple-element.46) | copy-start | bytes 1540
  347.1 74.9 %copy-start.14 = (f32[4,128]{1,0:T(4,128)S(1)}, f32[4,128]{1,0:T(4,128)}, u32[]{:S(2)}) copy-start(f32[4,128]{1,0:T(4,128)} %param.23) | copy-start | bytes 6148
  347.1 75.3 %copy-start.1 = (f32[80,24,128]{2,0,1:T(8,128)S(1)}, f32[80,24,128]{2,0,1:T(8,128)}, u32[]{:S(2)}) copy-start(f32[80,24,128]{2,0,1:T(8,128)} %copy-done) | copy-start | bytes 2949124
where the time goes:
time: 432 us; the launch traced here: 428 us
  blocking collectives  163 us (38%)
  other arithmetic  145 us (34%)
  waiting for transfers between devices  43.8 us (10%)
  local copies, waits for them, and re-layouts  41.1 us (10%)
  matrix products  23.1 us (5%)
  starting transfers between devices  11.3 us (3%)
    psum x4, blocking collectives, shards(): lax.psum(local_prior(existing_grid_values, obs_rows[batch_index], obs_col...  163 us
    another operation x12, other arithmetic, obs_factors(): factor = jnp.linalg.cholesky(covariance)  49.7 us
    another operation x8, other arithmetic, obs_factors(): lax.linalg.triangular_solve(factor, midpoint_values, left_side=True, lowe...  42.2 us
    another operation x4, other arithmetic, obs_factors(): lax.linalg.triangular_solve(shifted, anomaly, left_side=True, lower=True)  39.2 us
    ppermute x1, waiting for transfers between devices, padded_2(): before = lax.ppermute(last, axis, up)  32.9 us
    unnamed x64, local copies, waits for them, and re-layouts  17.7 us
    all_to_all x1, waiting for transfers between devices, shards(): lax.all_to_all(propagated_grids, 'mem', split_axis=3, concat_axis=0, tile...  10.9 us
    dot_general x4, matrix products, apply_update(): jnp.einsum('mrcx,km->rcxk', anomaly, obs_anomaly, precision=highest)  10.5 us
  transfers between devices with their start and end apart: 3, of which 2 were waited for; matrix products, arithmetic and copies ran while one was open for 2% of the time, Pallas kernels for 0%

commit v1 on v0

--- a/solution.py
+++ b/solution.py
@@ -4,6 +4,29 @@
 from jax.sharding import PartitionSpec as P
 
 highest = lax.Precision.HIGHEST
+
+
+def cut_along(x, dim, size):
+    shape = x.shape
+    pieces = x.reshape(*shape[:dim], size, shape[dim] // size, *shape[dim + 1 :])
+    return jnp.moveaxis(pieces, dim, 0)
+
+
+def joined_along(parts, dim):
+    shape = list(parts.shape[1:])
+    shape[dim] *= parts.shape[0]
+    return jnp.moveaxis(parts, 0, dim).reshape(shape)
+
+
+def exchange_directly(array, axis, split_dim, concat_dim):
+    size, position = (lax.axis_size(axis), lax.axis_index(axis))
+    parts = cut_along(array, split_dim, size)
+    outs = [parts[position]]
+    for step in range(1, size):
+        sent = parts[(position + step) % size]
+        outs.append(lax.ppermute(sent, axis, [(i, (i + step) % size) for i in range(size)]))
+    parts = jnp.stack(outs)[(position - jnp.arange(size)) % size]
+    return joined_along(parts, concat_dim)
 
 
 def padded_2(shard, sides, width):
@@ -131,9 +154,7 @@
         courant_y[:, None, :],
         diffusion[:, None, :],
     )
-    existing_grid_values = lax.all_to_all(
-        propagated_grids, "mem", split_axis=3, concat_axis=0, tiled=True
-    )
+    existing_grid_values = exchange_directly(propagated_grids, "mem", 3, 0)
     row_ids = row_start + jnp.arange(rows_dev, dtype=jnp.int32)
     col_ids = col_start + jnp.arange(cols_dev, dtype=jnp.int32)
     obs_rows = obs_cell // width

time: 432 us -> 404 us (0.935)
  local copies, waits for them, and re-layouts: 41.1 us -> 18.2 us
    unnamed x64 -> x56, local copies, waits for them, and re-layouts: 17.7 us -> 3.26 us
    all_to_all x1 -> x0, waiting for transfers between devices: 10.9 us -> none  [shards(): lax.all_to_all(propagated_grids, 'mem', split_axis=3, concat_axis=0, tile...]
    ppermute x0 -> x3, waiting for transfers between devices: none -> 9.65 us  [exchange_directly(): lax.ppermute(sent, axis, [(i, (i + step) % size) for i in range(size)])]
    all_to_all x4 -> x0, local copies, waits for them, and re-layouts: 6.76 us -> none  [shards(): lax.all_to_all(propagated_grids, 'mem', split_axis=3, concat_axis=0, tile...]
  transfers between devices with their start and end apart: 3 -> 5, of which waited for: 2 -> 4; matrix products, arithmetic and copies ran while one was open for 2% -> 3% of each run, Pallas kernels for 0% -> 0%
where the time goes in v1:
time: 404 us; the launch traced here: 398 us
  blocking collectives  164 us (41%)
  other arithmetic  141 us (35%)
  waiting for transfers between devices  41 us (10%)
  matrix products  23.2 us (6%)
  local copies, waits for them, and re-layouts  18.2 us (5%)
  starting transfers between devices  9.02 us (2%)
    psum x4, blocking collectives, shards(): lax.psum(local_prior(existing_grid_values, obs_rows[batch_index], obs_col...  164 us
    another operation x12, other arithmetic, obs_factors(): factor = jnp.linalg.cholesky(covariance)  49.7 us
    another operation x8, other arithmetic, obs_factors(): lax.linalg.triangular_solve(factor, midpoint_values, left_side=True, lowe...  42.1 us
    another operation x4, other arithmetic, obs_factors(): lax.linalg.triangular_solve(shifted, anomaly, left_side=True, lower=True)  39.2 us
    ppermute x1, waiting for transfers between devices, padded_2(): before = lax.ppermute(last, axis, up)  31.4 us
    dot_general x4, matrix products, apply_update(): jnp.einsum('mrcx,km->rcxk', anomaly, obs_anomaly, precision=highest)  10.5 us
    ppermute x3, waiting for transfers between devices, exchange_directly(): lax.ppermute(sent, axis, [(i, (i + step) % size) for i in range(size)])  9.65 us
    dot_general x4, matrix products, apply_update(): jnp.einsum('rcxk,km->mrcx', gain, coeffs, precision=highest)  8.39 us
  transfers between devices with their start and end apart: 5, of which 4 were waited for; matrix products, arithmetic and copies ran while one was open for 3% of the time, Pallas kernels for 0%

profile of v1, /device:TPU:0, one launch (start us, length us, event | category | flops | bytes accessed | tf_op | source)
XLA Modules:
  0.0 397.9 jit_solution(12732306436222194960)
XLA Ops:
  0.0 5.9 %collective-permute-start = (f32[20,1,24,512]{3,2,1,0:T(8,128)}, f32[20,1,24,512]{3,2,1,0:T(8,128)}, u32[]{:S(2)}, u32[]{:S(2)}) collective-permute-start(f32[20,1,24,512]{3,2,1,0:T(8,128)} %param.18), channel_id=1, source_target_pairs={{0,1},{1,2},{2,3},{3,4},{4,5},{5,6},{6,7},{8,9},{9,10},{10,11},{11... | collective-permute-start | bytes 2949128 | tf_op jit(solution)/shard_map/ppermute | solution.py:39
  10.0 1.4 fusion.185
  16.0 31.4 %collective-permute-done = f32[20,1,24,512]{3,2,1,0:T(8,128)} collective-permute-done((f32[20,1,24,512]{3,2,1,0:T(8,128)}, f32[20,1,24,512]{3,2,1,0:T(8,128)}, u32[]{:S(2)}, u32[]{:S(2)}) %collective-permute-start) | collective-permute-done | bytes 983072 | tf_op jit(solution)/shard_map/ppermute | solution.py:39
  47.4 2.4 multiply_add_fusion
  51.2 1.5 collective-permute-start.3
  55.1 1.5 collective-permute-done.4
  56.6 8.1 %collective-permute-done.3 = f32[20,1,24,128]{3,2,0,1:T(8,128)S(1)} collective-permute-done((f32[20,1,24,128]{3,2,0,1:T(8,128)S(1)}, f32[20,1,24,128]{3,2,0,1:T(8,128)S(1)}, u32[]{:S(2)}, u32[]{:S(2)}) %collective-permute-start.3) | collective-permute-done | bytes 245792 | tf_op jit(solution)/shard_map/ppermute | solution.py:27
  67.2 1.4 multiply_reduce_fusion.3
  68.8 42.1 %psum.28 = f32[128,80]{0,1:T(8,128)S(1)} all-reduce(f32[128,80]{0,1:T(8,128)S(1)} %broadcast_select_fusion.3), channel_id=1, replica_groups=mesh['mem'=4,'sub'=8] {'mem','sub'}, use_global_device_ids=true, to_apply=%region_0.1 | all-reduce | flops 10240 | bytes 81920 | tf_op jit(solution)/shard_map/psum | solution.py:173
  111.5 11.7 %cholesky.74 = f32[128,128]{1,0:T(8,128)S(1)} custom-call(f32[128,128]{1,0:T(8,128)S(1)} %copy.43), custom_call_target="Cholesky" | custom-call | tf_op jit(solution)/shard_map/jit(cholesky)/cholesky | solution.py:92
  124.7 9.8 %custom-call.36 = f32[1,128,128]{1,2,0:T(8,128)S(1)} custom-call(f32[1,128,128]{2,1,0:T(8,128)S(1)} %get-tuple-element.25), custom_call_target="InvertDiagBlocksLowerTriangular" | custom-call | tf_op jit(solution)/shard_map/triangular_solve/custom-call.3 | solution.py:99
  134.7 9.8 %custom-call.35 = f32[1,128,128]{1,2,0:T(8,128)S(1)} custom-call(f32[1,128,128]{2,1,0:T(8,128)S(1)} %get-tuple-element.24), custom_call_target="InvertDiagBlocksLowerTriangular" | custom-call | tf_op jit(solution)/shard_map/triangular_solve/custom-call.2 | solution.py:95
  145.0 2.6 fusion.31
  147.9 2.8 fusion.188
  153.2 41.4 %psum.29 = f32[128,80]{0,1:T(8,128)S(1)} all-reduce(f32[128,80]{0,1:T(8,128)S(1)} %broadcast_select_fusion.2), channel_id=1, replica_groups=mesh['mem'=4,'sub'=8] {'mem','sub'}, use_global_device_ids=true, to_apply=%region_5.11 | all-reduce | flops 10240 | bytes 81920 | tf_op jit(solution)/shard_map/psum | solution.py:173
  195.1 11.7 %cholesky.85 = f32[128,128]{1,0:T(8,128)S(1)} custom-call(f32[128,128]{1,0:T(8,128)S(1)} %copy.48), custom_call_target="Cholesky" | custom-call | tf_op jit(solution)/shard_map/jit(cholesky)/cholesky | solution.py:92
  208.1 9.8 %custom-call.40 = f32[1,128,128]{1,2,0:T(8,128)S(1)} custom-call(f32[1,128,128]{2,1,0:T(8,128)S(1)} %get-tuple-element.23), custom_call_target="InvertDiagBlocksLowerTriangular" | custom-call | tf_op jit(solution)/shard_map/triangular_solve/custom-call.3 | solution.py:99
  218.1 9.8 %custom-call.39 = f32[1,128,128]{1,2,0:T(8,128)S(1)} custom-call(f32[1,128,128]{2,1,0:T(8,128)S(1)} %get-tuple-element.22), custom_call_target="InvertDiagBlocksLowerTriangular" | custom-call | tf_op jit(solution)/shard_map/triangular_solve/custom-call.2 | solution.py:95
  228.3 2.6 fusion.37
  231.2 1.9 fusion.189
  235.6 39.5 %psum.30 = f32[128,80]{0,1:T(8,128)S(1)} all-reduce(f32[128,80]{0,1:T(8,128)S(1)} %broadcast_select_fusion.1), channel_id=1, replica_groups=mesh['mem'=4,'sub'=8] {'mem','sub'}, use_global_device_ids=true, to_apply=%region_8.14 | all-reduce | flops 10240 | bytes 81920 | tf_op jit(solution)/shard_map/psum | solution.py:173
  275.6 11.7 %cholesky.96 = f32[128,128]{1,0:T(8,128)S(1)} custom-call(f32[128,128]{1,0:T(8,128)S(1)} %copy.51), custom_call_target="Cholesky" | custom-call | tf_op jit(solution)/shard_map/jit(cholesky)/cholesky | solution.py:92
  288.7 9.8 %custom-call.44 = f32[1,128,128]{1,2,0:T(8,128)S(1)} custom-call(f32[1,128,128]{2,1,0:T(8,128)S(1)} %get-tuple-element.21), custom_call_target="InvertDiagBlocksLowerTriangular" | custom-call | tf_op jit(solution)/shard_map/triangular_solve/custom-call.3 | solution.py:99
  298.7 9.8 %custom-call.43 = f32[1,128,128]{1,2,0:T(8,128)S(1)} custom-call(f32[1,128,128]{2,1,0:T(8,128)S(1)} %get-tuple-element.20), custom_call_target="InvertDiagBlocksLowerTriangular" | custom-call | tf_op jit(solution)/shard_map/triangular_solve/custom-call.2 | solution.py:95
  309.0 2.6 fusion.35
  311.9 1.9 fusion.190
  316.3 41.4 %psum.31 = f32[128,80]{0,1:T(8,128)S(1)} all-reduce(f32[128,80]{0,1:T(8,128)S(1)} %broadcast_select_fusion), channel_id=1, replica_groups=mesh['mem'=4,'sub'=8] {'mem','sub'}, use_global_device_ids=true, to_apply=%region_11.17 | all-reduce | flops 10240 | bytes 81920 | tf_op jit(solution)/shard_map/psum | solution.py:173
  358.2 11.7 %cholesky.107 = f32[128,128]{1,0:T(8,128)S(1)} custom-call(f32[128,128]{1,0:T(8,128)S(1)} %copy.54), custom_call_target="Cholesky" | custom-call | tf_op jit(solution)/shard_map/jit(cholesky)/cholesky | solution.py:92
  371.4 9.8 %custom-call.48 = f32[1,128,128]{1,2,0:T(8,128)S(1)} custom-call(f32[1,128,128]{2,1,0:T(8,128)S(1)} %get-tuple-element.19), custom_call_target="InvertDiagBlocksLowerTriangular" | custom-call | tf_op jit(solution)/shard_map/triangular_solve/custom-call.3 | solution.py:99
  381.4 9.8 %custom-call.47 = f32[1,128,128]{1,2,0:T(8,128)S(1)} custom-call(f32[1,128,128]{2,1,0:T(8,128)S(1)} %get-tuple-element.18), custom_call_target="InvertDiagBlocksLowerTriangular" | custom-call | tf_op jit(solution)/shard_map/triangular_solve/custom-call.2 | solution.py:95
  391.7 2.6 fusion.33
  394.6 1.7 fusion.20
  (158 shorter events, 34.4 us)
Async XLA Ops:
  0.0 15.6 %copy-start.8 = (f32[20,1,24,512]{3,2,1,0:T(8,128)S(1)}, f32[20,1,24,512]{3,2,1,0:T(8,128)}, u32[]{:S(2)}) copy-start(f32[20,1,24,512]{3,2,1,0:T(8,128)} %param.18) | copy-start | bytes 2949124
  0.0 47.4 %collective-permute-start = (f32[20,1,24,512]{3,2,1,0:T(8,128)}, f32[20,1,24,512]{3,2,1,0:T(8,128)}, u32[]{:S(2)}, u32[]{:S(2)}) collective-permute-start(f32[20,1,24,512]{3,2,1,0:T(8,128)} %param.18), channel_id=1, source_target_pairs={{0,1},{1,2},{2,3},{3,4},{4,5},{5,6},{6,7},{8,9},{9,10},{10,11},{11... | collective-permute-start | bytes 2949128 | tf_op jit(solution)/shard_map/ppermute | solution.py:39
  5.9 41.4 %collective-permute-start.1 = (f32[20,1,24,512]{3,2,1,0:T(8,128)}, f32[20,1,24,512]{3,2,1,0:T(8,128)}, u32[]{:S(2)}, u32[]{:S(2)}) collective-permute-start(f32[20,1,24,512]{3,2,1,0:T(8,128)} %param.18), channel_id=1, source_target_pairs={{1,0},{2,1},{3,2},{4,3},{5,4},{6,5},{7,6},{9,8},{10,9},{11,10},{12... | collective-permute-start | bytes 2949128 | tf_op jit(solution)/shard_map/ppermute | solution.py:40
  15.6 31.7 %copy-start.13 = (f32[1,512]{1,0:T(1,128)S(1)}, f32[1,512]{1,0:T(1,128)}, u32[]{:S(2)}) copy-start(f32[1,512]{1,0:T(1,128)} %param.21) | copy-start | bytes 6148
  51.1 5.5 %collective-permute-start.4 = (f32[20,1,24,128]{3,2,0,1:T(8,128)S(1)}, f32[20,1,24,128]{3,2,0,1:T(8,128)S(1)}, u32[]{:S(2)}, u32[]{:S(2)}) collective-permute-start(f32[20,1,24,128]{3,2,0,1:T(8,128)S(1)} %bitcast.355), channel_id=1, source_target_pairs={{0,24},{8,0},{16,8},{24,16},{1,25},{9,1},{17,9},{25,17},{2,26},{10... | collective-permute-start | bytes 737288 | tf_op jit(solution)/shard_map/ppermute | solution.py:27
  51.2 13.4 %collective-permute-start.3 = (f32[20,1,24,128]{3,2,0,1:T(8,128)S(1)}, f32[20,1,24,128]{3,2,0,1:T(8,128)S(1)}, u32[]{:S(2)}, u32[]{:S(2)}) collective-permute-start(f32[20,1,24,128]{3,2,0,1:T(8,128)S(1)} %bitcast.353), channel_id=1, source_target_pairs={{0,16},{8,24},{16,0},{24,8},{1,17},{9,25},{17,1},{25,9},{2,18},{10... | collective-permute-start | bytes 737288 | tf_op jit(solution)/shard_map/ppermute | solution.py:27
  52.7 12.0 %collective-permute-start.2 = (f32[20,1,24,128]{3,2,0,1:T(8,128)S(1)}, f32[20,1,24,128]{3,2,0,1:T(8,128)S(1)}, u32[]{:S(2)}, u32[]{:S(2)}) collective-permute-start(f32[20,1,24,128]{3,2,0,1:T(8,128)S(1)} %bitcast.352), channel_id=1, source_target_pairs={{0,8},{8,16},{16,24},{24,0},{1,9},{9,17},{17,25},{25,1},{2,10},{10... | collective-permute-start | bytes 737288 | tf_op jit(solution)/shard_map/ppermute | solution.py:27
  65.4 0.9 copy-start
  67.2 1.6 copy-start.17
  67.2 43.7 %copy-start.1 = (f32[4,20,24,128]{3,2,1,0:T(8,128)S(1)}, f32[4,20,24,128]{3,2,1,0:T(8,128)}, u32[]{:S(2)}) copy-start(f32[4,20,24,128]{3,2,1,0:T(8,128)} %copy-done) | copy-start | bytes 2949124
  67.2 43.8 %copy-start.25 = (f32[128]{0:T(128)S(1)}, f32[128]{0:T(128)}, u32[]{:S(2)}) copy-start(f32[128]{0:T(128)} %get-tuple-element.56) | copy-start | bytes 1540
  67.2 56.7 %copy-start.24 = (f32[128]{0:T(128)S(1)}, f32[128]{0:T(128)}, u32[]{:S(2)}) copy-start(f32[128]{0:T(128)} %get-tuple-element.53) | copy-start | bytes 1540
  68.7 75.8 %copy-start.11 = (f32[4,128]{1,0:T(4,128)S(1)}, f32[4,128]{1,0:T(4,128)}, u32[]{:S(2)}) copy-start(f32[4,128]{1,0:T(4,128)} %param.23) | copy-start | bytes 6148
  150.7 0.9 copy-start.4
  151.7 0.8 copy-start.9
  152.5 0.7 copy-start.16
  152.5 42.1 %copy-start.23 = (f32[128]{0:T(128)S(1)}, f32[128]{0:T(128)}, u32[]{:S(2)}) copy-start(f32[128]{0:T(128)} %get-tuple-element.55) | copy-start | bytes 1540
  152.5 55.0 %copy-start.22 = (f32[128]{0:T(128)S(1)}, f32[128]{0:T(128)}, u32[]{:S(2)}) copy-start(f32[128]{0:T(128)} %get-tuple-element.52) | copy-start | bytes 1540
  152.5 75.8 %copy-start.10 = (f32[24,128]{1,0:T(8,128)S(1)}, f32[24,128]{1,0:T(8,128)}, u32[]{:S(2)}) copy-start(f32[24,128]{1,0:T(8,128)} %get-tuple-element.68) | copy-start | bytes 36868
  152.5 75.8 %copy-start.5 = (f32[80,24,128]{2,0,1:T(8,128)S(1)}, f32[80,24,128]{2,0,1:T(8,128)}, u32[]{:S(2)}) copy-start(f32[80,24,128]{2,0,1:T(8,128)} %copy-done.4) | copy-start | bytes 2949124
  233.1 0.9 copy-start.6
  234.9 0.7 copy-start.15
  234.9 40.2 %copy-start.21 = (f32[128]{0:T(128)S(1)}, f32[128]{0:T(128)}, u32[]{:S(2)}) copy-start(f32[128]{0:T(128)} %get-tuple-element.57) | copy-start | bytes 1540
  234.9 53.1 %copy-start.20 = (f32[128]{0:T(128)S(1)}, f32[128]{0:T(128)}, u32[]{:S(2)}) copy-start(f32[128]{0:T(128)} %get-tuple-element.51) | copy-start | bytes 1540
  234.9 74.0 %copy-start.7 = (f32[80,24,128]{2,0,1:T(8,128)S(1)}, f32[80,24,128]{2,0,1:T(8,128)}, u32[]{:S(2)}) copy-start(f32[80,24,128]{2,0,1:T(8,128)} %copy-done.6) | copy-start | bytes 2949124
  313.8 0.9 copy-start.2
  315.6 0.7 copy-start.14
  315.6 42.1 %copy-start.19 = (f32[128]{0:T(128)S(1)}, f32[128]{0:T(128)}, u32[]{:S(2)}) copy-start(f32[128]{0:T(128)} %get-tuple-element.54) | copy-start | bytes 1540
  315.6 55.1 %copy-start.18 = (f32[128]{0:T(128)S(1)}, f32[128]{0:T(128)}, u32[]{:S(2)}) copy-start(f32[128]{0:T(128)} %get-tuple-element.50) | copy-start | bytes 1540
  315.6 75.7 %copy-start.12 = (f32[4,128]{1,0:T(4,128)S(1)}, f32[4,128]{1,0:T(4,128)}, u32[]{:S(2)}) copy-start(f32[4,128]{1,0:T(4,128)} %param.23) | copy-start | bytes 6148
  315.6 76.0 %copy-start.3 = (f32[80,24,128]{2,0,1:T(8,128)S(1)}, f32[80,24,128]{2,0,1:T(8,128)}, u32[]{:S(2)}) copy-start(f32[80,24,128]{2,0,1:T(8,128)} %copy-done.2) | copy-start | bytes 2949124
